TPU v7x, 32 devices: a whole 2x2x4 slice. The times are simulated.
32 devices in a mesh: dp: 4 (over x, core), tensor: 2 (over y), layer: 4 (over z).
Axes of the slice: x: 2, y: 2, z: 4, core: 2. Of those that a mesh axis runs over, the one named last changes fastest.
Arguments:
- saved_inputs: bfloat16 [4, 2048, 8192], P(None, 'dp', ('tensor', 'layer')), may hold values from -6 to 6
- output_grad: bfloat16 [2048, 8192], P('dp', ('tensor', 'layer')), may hold values from -4 to 4
- weights: bfloat16 [4, 8192, 2, 4, 1024], P(None, 'tensor', None, 'layer'), may hold values from -0.0625 to 0.0625
- proj_in: bfloat16 [4, 64, 8192], P(None, None, ('tensor', 'layer')), may hold values from -0.0625 to 0.0625
- proj_out: bfloat16 [4, 64, 8192], P(None, None, ('tensor', 'layer')), may hold values from -0.0625 to 0.0625
- query_grads: bfloat16 [4, 1024, 4096], P('layer', ('dp', 'tensor')), may hold values from -0.00390625 to 0.00390625
- owner_map: int32 [4], replicated, may hold values from 0 to 3, each once
Outputs:
- input_grad: bfloat16 [2048, 8192], P('dp', ('tensor', 'layer'))
- scores: float32 [4, 1024], P('layer', ('dp', 'tensor'))
Inputs may be any that keep to these rules, and one draw needn't show every extreme that they name: `owner_map`: each owner is named by exactly one layer.
All inputs are finite; a program needn't handle non-finite values.
Results may differ from a plain program's by a relative error of at most 0.035.
Values may be sent and summed in bfloat16 or wider, within the bound.
A program may use at most 256 MiB of HBM per device.

v0:
```python
import functools

import jax
import jax.numpy as jnp
from jax import lax
from jax.experimental import pallas as pl
from jax.experimental.pallas import tpu as pltpu
from jax.sharding import PartitionSpec as P

LEN = 512
CHUNKS = 2
MESH = pl.DeviceIdType.MESH
VMEM_BYTES = 67_000_000


def stack_kernel(
    dims,
    grad_hbm,
    weight_hbm,
    proj_ref,
    out_hbm,
    factor_ref,
    raw,
    flat,
    feats,
    part,
    from_left,
    from_right,
    total,
    raw_sem,
    io_sem,
    feat_send,
    feat_recv,
    part_send,
    left_recv,
    right_recv,
):
    layers, n_layer, n_tensor, rows, width, block = dims
    last = n_layer - 1
    piece_rows = flat.shape[2]
    blocks = piece_rows // block
    per_level = n_layer * blocks
    n_tile = min(512, piece_rows)
    z = lax.axis_index("layer")
    t = lax.axis_index("tensor")

    def nth_piece(i):
        return jnp.where(2 * z < n_layer, last - i, i)

    def raw_copy(n):
        level = layers - 1 - n // per_level
        i = (n // blocks) % n_layer
        start = pl.multiple_of(nth_piece(i) * piece_rows + (n % blocks) * block, block)
        return pltpu.make_async_copy(
            weight_hbm.at[level, pl.ds(start, block)], raw.at[n % 2], raw_sem.at[n % 2]
        )

    def relay(first, count):
        @pl.loop(first, first + count)
        def _(n):
            raw_copy(n).wait()

            @pl.when(n + 1 < layers * per_level)
            def _():
                raw_copy(n + 1).start()

            level = layers - 1 - n // per_level
            q = nth_piece((n // blocks) % n_layer)
            at = pl.ds(pl.multiple_of((n % blocks) * block, block), block)
            for a in range(n_tensor):
                flat[level % 2, q, at, a * width : (a + 1) * width] = raw[n % 2, :, a, :]

    def feat_copy(level, c, shift):
        return pltpu.make_async_remote_copy(
            src_ref=feats.at[level, c, t],
            dst_ref=feats.at[level, c, t],
            send_sem=feat_send.at[level, c, shift - 1],
            recv_sem=feat_recv.at[level, c, shift - 1],
            device_id={"tensor": lax.rem(t + shift, n_tensor)},
            device_id_type=MESH,
        )

    def right_copy(level, c, q):
        return pltpu.make_async_remote_copy(
            src_ref=part.at[c, q],
            dst_ref=from_left.at[level % 2, c, last - q],
            send_sem=part_send.at[c, q],
            recv_sem=left_recv.at[level % 2, c, last - q],
            device_id={"layer": z + 1},
            device_id_type=MESH,
        )

    def left_copy(level, c, q):
        return pltpu.make_async_remote_copy(
            src_ref=part.at[c, q],
            dst_ref=from_right.at[level % 2, c, q],
            send_sem=part_send.at[c, q],
            recv_sem=right_recv.at[level % 2, c, q],
            device_id={"layer": z - 1},
            device_id_type=MESH,
        )

    def wait_part_sends(c):
        for q in range(n_layer):

            if q > 0:

                @pl.when(q > z)
                def _():
                    right_copy(0, c, q).wait_send()

            if q < last:

                @pl.when(q < z)
                def _():
                    left_copy(0, c, q).wait_send()

    def multiply(level, c, i):
        q = nth_piece(i)

        @pl.loop(0, piece_rows // n_tile)
        def _(j):
            at = pl.ds(pl.multiple_of(j * n_tile, n_tile), n_tile)
            acc = None
            for a in range(n_tensor):
                term = lax.dot_general(
                    feats[level, c, a],
                    flat[level % 2, q, at, a * width : (a + 1) * width],
                    (((1,), (1,)), ((), ())),
                    preferred_element_type=jnp.float32,
                )
                acc = term if acc is None else acc + term
            part[c, q, :, at] = acc.astype(jnp.bfloat16)

        @pl.when((z == 0) & (q > 0))
        def _():
            right_copy(level, c, q).start()

        @pl.when((z == last) & (q < last))
        def _():
            left_copy(level, c, q).start()

    def forward(level, c, s):
        right_piece, left_piece = last - s + z, s - last + z

        @pl.when((z > 0) & (right_piece <= last))
        def _():
            right_copy(level, c, right_piece).wait_recv()

            @pl.when(right_piece > z)
            def _():
                part[c, right_piece] = (
                    part[c, right_piece].astype(jnp.float32)
                    + from_left[level % 2, c, last - right_piece].astype(jnp.float32)
                ).astype(jnp.bfloat16)
                right_copy(level, c, right_piece).start()

        @pl.when((z < last) & (left_piece >= 0))
        def _():
            left_copy(level, c, left_piece).wait_recv()

            @pl.when(left_piece < z)
            def _():
                part[c, left_piece] = (
                    part[c, left_piece].astype(jnp.float32)
                    + from_right[level % 2, c, left_piece].astype(jnp.float32)
                ).astype(jnp.bfloat16)
                left_copy(level, c, left_piece).start()

    def out_copy(c):
        return pltpu.make_async_copy(
            feats.at[0, c, t], out_hbm.at[pl.ds(c * rows, rows)], io_sem.at[c]
        )

    def finish(level, c):
        for shift in range(1, n_tensor):
            feat_copy(level, c, shift).wait_send()
        total[c] = total[c] + part[c, z].astype(jnp.float32)

        @pl.when(z > 0)
        def _():
            total[c] = total[c] + from_left[level % 2, c, last - z].astype(jnp.float32)

        @pl.when(z < last)
        def _():
            total[c] = total[c] + from_right[level % 2, c, z].astype(jnp.float32)

        feats[jnp.maximum(level - 1, 0), c, t] = total[c].astype(jnp.bfloat16)

        @pl.when(level > 0)
        def _():
            for shift in range(1, n_tensor):
                feat_copy(level - 1, c, shift).start()

        @pl.when(level == 0)
        def _():
            out_copy(c).start()

    barrier = pltpu.get_barrier_semaphore()
    for shift in range(1, n_tensor):
        pl.semaphore_signal(
            barrier, inc=1, device_id={"tensor": lax.rem(t + shift, n_tensor)}, device_id_type=MESH
        )

    @pl.when(z > 0)
    def _():
        pl.semaphore_signal(barrier, inc=1, device_id={"layer": z - 1}, device_id_type=MESH)

    @pl.when(z < last)
    def _():
        pl.semaphore_signal(barrier, inc=1, device_id={"layer": z + 1}, device_id_type=MESH)

    raw_copy(0).start()
    for c in range(CHUNKS):
        pltpu.make_async_copy(
            grad_hbm.at[pl.ds(c * rows, rows)], feats.at[layers - 1, c, t], io_sem.at[c]
        ).start()
    pl.semaphore_wait(barrier, n_tensor - 1 + jnp.minimum(z, 1) + jnp.minimum(last - z, 1))

    for c in range(CHUNKS):
        pltpu.make_async_copy(
            grad_hbm.at[pl.ds(c * rows, rows)], feats.at[layers - 1, c, t], io_sem.at[c]
        ).wait()
        for shift in range(1, n_tensor):
            feat_copy(layers - 1, c, shift).start()
        total[c] = feats[layers - 1, c, t].astype(jnp.float32)

    phases = layers * CHUNKS

    @pl.loop(0, phases + 1)
    def _(p):
        level = layers - 1 - p // CHUNKS
        c = p % CHUNKS
        old_level = layers - 1 - (p - 1) // CHUNKS
        old_c = (p + CHUNKS - 1) % CHUNKS

        @pl.when(p > 0)
        def _():
            forward(old_level, old_c, 1)

        @pl.when(p < phases)
        def _():
            @pl.when(p >= CHUNKS)
            def _():
                wait_part_sends(c)

            @pl.loop(0, n_layer)
            def _(i):
                @pl.when(p == 0)
                def _():
                    relay(i * blocks, blocks)

                @pl.when(i == 0)
                def _():
                    for shift in range(1, n_tensor):
                        feat_copy(level, c, shift).wait_recv()

                multiply(level, c, i)

        half = per_level // 2
        quarter = half // 2
        base = (layers - level) * per_level + c * half

        @pl.when((p > 0) & (level > 0) & (p < phases))
        def _():
            @pl.when(p == 1)
            def _():
                relay(per_level, half)

            relay(base, quarter)

        for s in range(2, n_layer - 1):

            @pl.when(p > 0)
            def _():
                forward(old_level, old_c, s)

        @pl.when((p > 0) & (level > 0) & (p < phases))
        def _():
            relay(base + quarter, half - quarter)

        @pl.when(p > 0)
        def _():
            forward(old_level, old_c, last)
            finish(old_level, old_c)

        @pl.when(p < phases)
        def _():
            factor_ref[level, pl.ds(pl.multiple_of(c * rows, rows), rows), :] = lax.dot_general(
                feats[level, c, t],
                proj_ref[level],
                (((1,), (1,)), ((), ())),
                preferred_element_type=jnp.float32,
            )

    for c in range(CHUNKS):
        wait_part_sends(c)
        out_copy(c).wait()


def backward_stack(output_grad, weights, proj_out):
    layers, in_rows, n_tensor, width = weights.shape
    tokens = output_grad.shape[0]
    rank = proj_out.shape[1]
    n_layer = lax.axis_size("layer")
    rows = tokens // CHUNKS
    piece_rows = in_rows // n_layer
    block = min(128, piece_rows)
    bf16, f32 = jnp.bfloat16, jnp.float32
    dma = pltpu.SemaphoreType.DMA
    hops = n_layer - 1
    return pl.pallas_call(
        functools.partial(stack_kernel, (layers, n_layer, n_tensor, rows, width, block)),
        out_shape=(
            jax.ShapeDtypeStruct((tokens, width), bf16),
            jax.ShapeDtypeStruct((layers, tokens, rank), f32),
        ),
        in_specs=[
            pl.BlockSpec(memory_space=pl.ANY),
            pl.BlockSpec(memory_space=pl.ANY),
            pl.BlockSpec(memory_space=pltpu.VMEM),
        ],
        out_specs=(pl.BlockSpec(memory_space=pl.ANY), pl.BlockSpec(memory_space=pltpu.VMEM)),
        scratch_shapes=[
            pltpu.VMEM((2, block, n_tensor, width), bf16),
            pltpu.VMEM((2, n_layer, piece_rows, n_tensor * width), bf16),
            pltpu.VMEM((layers, CHUNKS, n_tensor, rows, width), bf16),
            pltpu.VMEM((CHUNKS, n_layer, rows, piece_rows), bf16),
            pltpu.VMEM((2, CHUNKS, hops, rows, piece_rows), bf16),
            pltpu.VMEM((2, CHUNKS, hops, rows, piece_rows), bf16),
            pltpu.VMEM((CHUNKS, rows, width), f32),
            dma((2,)),
            dma((CHUNKS,)),
            dma((layers, CHUNKS, n_tensor - 1)),
            dma((layers, CHUNKS, n_tensor - 1)),
            dma((CHUNKS, n_layer)),
            dma((2, CHUNKS, hops)),
            dma((2, CHUNKS, hops)),
        ],
        compiler_params=pltpu.CompilerParams(
            collective_id=0, has_side_effects=True, vmem_limit_bytes=VMEM_BYTES
        ),
        name="backward_stack",
    )(output_grad, weights, proj_out)


def on_device(saved_inputs, output_grad, weights, proj_in, proj_out, query_grads, owner_map):
    layers = weights.shape[0]
    tok_rows = output_grad.shape[0]
    rank = proj_in.shape[1]
    n_tensor = lax.axis_size("tensor")
    n_layer = lax.axis_size("layer")
    owner = lax.axis_index("layer")
    input_grad, out_factor = backward_stack(output_grad, weights[:, :, :, 0, :], proj_out)
    in_factor = jnp.einsum(
        "ltd,lrd->ltr", saved_inputs, proj_in, preferred_element_type=jnp.float32
    )
    stacked = jnp.concatenate([out_factor, in_factor], axis=2).astype(jnp.bfloat16)
    layer_ids = jnp.arange(layers, dtype=jnp.int32)
    inverse = jnp.sum(
        layer_ids[None, :] * (owner_map[None, :] == layer_ids[:, None]).astype(jnp.int32), axis=1
    )
    sequences = tok_rows // LEN
    block_rows = tok_rows // n_tensor
    by_owner = jnp.take(stacked, inverse, axis=0).reshape(n_layer, n_tensor, block_rows, 2 * rank)
    ordered = jnp.swapaxes(by_owner, 0, 1).reshape(n_tensor * n_layer, block_rows, 2 * rank)
    mine = lax.psum_scatter(
        ordered, ("tensor", "layer"), scatter_dimension=0, tiled=True
    ).astype(jnp.float32)[0]
    first_row = lax.axis_index("tensor") * block_rows
    row_seq = (first_row + jnp.arange(block_rows, dtype=jnp.int32)) // LEN
    member = (row_seq[:, None] == jnp.arange(sequences, dtype=jnp.int32)[None, :]).astype(
        jnp.float32
    )
    partial_blocks = jnp.einsum(
        "rs,ra,rb->sab", member, mine[:, :rank], mine[:, rank:], precision=lax.Precision.HIGHEST
    )
    blocks = lax.psum(partial_blocks.reshape(sequences, rank * rank), "tensor")
    blocks_bf = blocks.astype(jnp.bfloat16)
    queries = query_grads[0]
    partial_scores = jnp.einsum(
        "er,qr->eq",
        lax.all_gather(blocks_bf, "dp", axis=0, tiled=True),
        queries,
        preferred_element_type=jnp.float32,
    )
    total = lax.psum(partial_scores, "layer")
    kept = total.shape[0] // n_layer
    scores = lax.dynamic_slice_in_dim(total, owner * kept, kept, 0)
    return (input_grad, scores)


def solution(mesh):
    in_specs = (
        P(None, "dp", ("tensor", "layer")),
        P("dp", ("tensor", "layer")),
        P(None, "tensor", None, "layer", None),
        P(None, None, ("tensor", "layer")),
        P(None, None, ("tensor", "layer")),
        P("layer", ("dp", "tensor"), None),
        P(),
    )
    out_specs = (P("dp", ("tensor", "layer")), P("layer", ("dp", "tensor")))
    return jax.shard_map(
        on_device, mesh=mesh, in_specs=in_specs, out_specs=out_specs, check_vma=False
    )
```

profile of v0, /device:TPU:0, one launch (start us, length us, event | category | flops | bytes accessed | tf_op | source)
XLA Modules:
  0.0 433.7 jit_solution(12929532589711100190)
XLA Ops:
  7.2 0.0 reduce-scatter.2.cloned.1.call-start
  7.2 0.8 select_reduce_fusion
  8.0 320.5 %backward_stack.1 = (bf16[512,1024]{1,0:T(8,128)(2,1)}, f32[4,512,64]{2,1,0:T(8,128)}) custom-call(bf16[512,1024]{1,0:T(8,128)(2,1)} %grad_hbm.1, bf16[4,4096,2,1024]{3,2,1,0:T(2,128)(2,1)} %bitcast.weight_hbm, bf16[4,64,1024]{2,1,0:T(8,128)(2,1)} %proj_ref.1), custom_call_target="tpu_custom_call" | custom-call | tf_op jit(solution)/shard_map/backward_stack/pallas_call | solution.py:312
  328.5 1.3 convert.10
  329.8 0.0 copy-start
  329.8 3.8 convolution_convert_fusion
  333.6 0.3 copy.16
  333.9 0.3 pad_maximum_fusion
  334.2 0.6 gather_fusion
  334.8 0.9 copy_select_fusion
  335.7 0.0 reduce-scatter.2.cloned.1.call-update
  335.8 61.6 %reduce-scatter.2.cloned.1.call-done = bf16[1,256,128]{2,1,0:T(8,128)(2,1)} async-done(((bf16[8,256,128]{2,1,0:T(8,128)(2,1)}), bf16[1,256,128]{2,1,0:T(8,128)(2,1)}) %reduce-scatter.2.cloned.1.call-update) | async-done | bytes 65552 | tf_op jit(solution)/shard_map/reduce_scatter | solution.py:367
  397.3 1.2 fusion.2
  398.6 0.1 transpose.10
  398.7 9.4 %psum.14 = bf16[1,4096]{1,0:T(2,128)(2,1)S(1)} all-reduce(f32[1,4096]{1,0:T(1,128)S(1)} %transpose.10), channel_id=1, replica_groups=mesh['dp'=4,'tensor'=2,'layer'=4] {'tensor'}, use_global_device_ids=true, to_apply=%region_2.3 | all-reduce | flops 4096 | bytes 24576 | tf_op jit(solution)/shard_map/psum | solution.py:378
  408.1 5.2 %all-gather = bf16[4,1,4096]{2,1,0:T(2,128)(2,1)S(1)} all-gather(bf16[1,1,4096]{2,1,0:T(2,128)(2,1)S(1)} %bitcast.23), channel_id=1, replica_groups=mesh['dp'=4,'tensor'=2,'layer'=4] {'dp'}, dimensions={0}, use_global_device_ids=true | all-gather | bytes 40960 | tf_op jit(solution)/shard_map/all_gather | solution.py:383
  413.3 0.0 copy-done
  413.3 0.4 fusion
  413.7 10.3 %psum.15 = f32[4,128]{1,0:T(4,128)S(1)} all-reduce(f32[4,128]{1,0:T(4,128)S(1)} %fusion), channel_id=1, replica_groups=mesh['dp'=4,'tensor'=2,'layer'=4] {'layer'}, use_global_device_ids=true, to_apply=%region_3.4 | all-reduce | flops 512 | bytes 4096 | tf_op jit(solution)/shard_map/psum | solution.py:387
  424.0 0.5 constant_dynamic-slice_fusion
  424.6 2.3 copy.25
  (4 shorter events, 0.0 us)
Async XLA Ops:
  7.2 390.2 %reduce-scatter.2.cloned.1.call-start = ((), (), s32[]{:S(2)}) async-start(), calls=%async_computation.1 | async-start | bytes 589824 | tf_op jit(solution)/shard_map/reduce_scatter | solution.py:367
  329.8 83.6 %copy-start = (bf16[1,128,4096]{2,1,0:T(8,128)(2,1)S(1)}, bf16[1,128,4096]{2,1,0:T(8,128)(2,1)}, u32[]{:S(2)}) copy-start(bf16[1,128,4096]{2,1,0:T(8,128)(2,1)} %param.12) | copy-start | bytes 3145732
Sparse Core Ops, SparseCore 0:
  335.9 61.4 reduce-scatter.1
where the time goes:
time: 434 us
  Pallas kernels  320 us (74%)
  waiting for transfers between devices  61.6 us (14%)
  blocking collectives  25 us (6%)
  between operations  14.1 us (3%)
  matrix products  5.4 us (1%)
    pallas_call x1, Pallas kernels, backward_stack(): pl.pallas_call(functools.partial(stack_kernel, (layers, n_layer, n_tensor...  320 us
    reduce_scatter x1, waiting for transfers between devices, on_device(): lax.psum_scatter(ordered, ('tensor', 'layer'), scatter_dimension=0, tiled...  61.6 us
    psum x1, blocking collectives, on_device(): total = lax.psum(partial_scores, 'layer')  10.3 us
    psum x1, blocking collectives, on_device(): blocks = lax.psum(partial_blocks.reshape(sequences, rank * rank), 'tensor')  9.4 us
  transfers between devices with their start and end apart: 1, of which 1 were waited for; matrix products, arithmetic and copies ran while one was open for 0% of the time, Pallas kernels for 0%

commit v1 on v0

v1 whole, which is shorter than its diff:
```python
import functools

import jax
import jax.numpy as jnp
from jax import lax
from jax.experimental import pallas as pl
from jax.experimental.pallas import tpu as pltpu
from jax.sharding import PartitionSpec as P

LEN = 512
CHUNKS = 4
RAW = 3
MESH = pl.DeviceIdType.MESH
VMEM_BYTES = 67_000_000
NT = (((1,), (1,)), ((), ()))
NN = (((1,), (0,)), ((), ()))


def stack_kernel(
    dims,
    owner_ref,
    grad_hbm,
    weight_hbm,
    saved_hbm,
    proj_in_hbm,
    proj_out_hbm,
    query_hbm,
    out_hbm,
    score_ref,
    raw,
    flat,
    feats,
    part,
    from_left,
    from_right,
    total,
    proj_in,
    proj_out,
    queries,
    saved,
    out_factor,
    in_mine,
    in_peer,
    in_sum,
    run_send,
    run_recv,
    in_total,
    block,
    level_blocks,
    owner_send,
    owner_recv,
    tensor_send,
    tensor_recv,
    seq_blocks,
    score_send,
    score_recv,
    raw_sem,
    io_sem,
    load_sem,
    feat_send,
    feat_recv,
    part_send,
    left_recv,
    right_recv,
    in_send_sem,
    in_recv_sem,
    run_send_sem,
    run_recv_sem,
    gather_send_sem,
    gather_recv_sem,
    owner_send_sem,
    owner_recv_sem,
    tensor_send_sem,
    tensor_recv_sem,
    seq_send_sem,
    seq_recv_sem,
    score_send_sem,
    score_recv_sem,
):
    layers, n_layer, n_tensor, n_dp, rows, width, rank, step = dims
    last = n_layer - 1
    f32, bf16 = jnp.float32, jnp.bfloat16
    piece_rows = flat.shape[2]
    blocks = piece_rows // step
    per_level = n_layer * blocks
    n_tile = min(512, piece_rows)
    tokens = rows * CHUNKS
    share = tokens // n_tensor
    lanes = 2 * rank
    z = lax.axis_index("layer")
    t = lax.axis_index("tensor")
    d = lax.axis_index("dp")

    def nth_piece(i):
        return jnp.where(2 * z < n_layer, last - i, i)

    def raw_copy(n):
        level = layers - 1 - n // per_level
        i = (n // blocks) % n_layer
        start = pl.multiple_of(nth_piece(i) * piece_rows + (n % blocks) * step, step)
        return pltpu.make_async_copy(
            weight_hbm.at[level, pl.ds(start, step)], raw.at[n % RAW], raw_sem.at[n % RAW]
        )

    def relay(first, count):
        @pl.loop(first, first + count)
        def _(n):
            raw_copy(n).wait()

            @pl.when(n + RAW - 1 < layers * per_level)
            def _():
                raw_copy(n + RAW - 1).start()

            level = layers - 1 - n // per_level
            q = nth_piece((n // blocks) % n_layer)
            at = pl.ds(pl.multiple_of((n % blocks) * step, step), step)
            for a in range(n_tensor):
                flat[level % 2, q, at, a * width : (a + 1) * width] = raw[n % RAW, :, a, :]

    def feat_copy(level, c, shift):
        return pltpu.make_async_remote_copy(
            src_ref=feats.at[level % 2, c, t],
            dst_ref=feats.at[level % 2, c, t],
            send_sem=feat_send.at[level % 2, c, shift - 1],
            recv_sem=feat_recv.at[level % 2, c, shift - 1],
            device_id={"tensor": lax.rem(t + shift, n_tensor)},
            device_id_type=MESH,
        )

    def right_copy(slot, level, c, q):
        return pltpu.make_async_remote_copy(
            src_ref=part.at[slot, q],
            dst_ref=from_left.at[level % 2, c, last - q],
            send_sem=part_send.at[slot, q],
            recv_sem=left_recv.at[level % 2, c, last - q],
            device_id={"layer": z + 1},
            device_id_type=MESH,
        )

    def left_copy(slot, level, c, q):
        return pltpu.make_async_remote_copy(
            src_ref=part.at[slot, q],
            dst_ref=from_right.at[level % 2, c, q],
            send_sem=part_send.at[slot, q],
            recv_sem=right_recv.at[level % 2, c, q],
            device_id={"layer": z - 1},
            device_id_type=MESH,
        )

    def wait_part_sends(slot):
        for q in range(n_layer):

            if q > 0:

                @pl.when(q > z)
                def _():
                    right_copy(slot, 0, 0, q).wait_send()

            if q < last:

                @pl.when(q < z)
                def _():
                    left_copy(slot, 0, 0, q).wait_send()

    def multiply(slot, level, c, i):
        q = nth_piece(i)

        @pl.loop(0, piece_rows // n_tile)
        def _(j):
            at = pl.ds(pl.multiple_of(j * n_tile, n_tile), n_tile)
            acc = None
            for a in range(n_tensor):
                term = lax.dot_general(
                    feats[level % 2, c, a],
                    flat[level % 2, q, at, a * width : (a + 1) * width],
                    NT,
                    preferred_element_type=f32,
                )
                acc = term if acc is None else acc + term
            part[slot, q, :, at] = acc.astype(bf16)

        @pl.when((z == 0) & (q > 0))
        def _():
            right_copy(slot, level, c, q).start()

        @pl.when((z == last) & (q < last))
        def _():
            left_copy(slot, level, c, q).start()

    def forward(slot, level, c, s):
        right_piece, left_piece = last - s + z, s - last + z

        @pl.when((z > 0) & (right_piece <= last))
        def _():
            right_copy(slot, level, c, right_piece).wait_recv()

            @pl.when(right_piece > z)
            def _():
                part[slot, right_piece] = (
                    part[slot, right_piece].astype(f32)
                    + from_left[level % 2, c, last - right_piece].astype(f32)
                ).astype(bf16)
                right_copy(slot, level, c, right_piece).start()

        @pl.when((z < last) & (left_piece >= 0))
        def _():
            left_copy(slot, level, c, left_piece).wait_recv()

            @pl.when(left_piece < z)
            def _():
                part[slot, left_piece] = (
                    part[slot, left_piece].astype(f32)
                    + from_right[level % 2, c, left_piece].astype(f32)
                ).astype(bf16)
                left_copy(slot, level, c, left_piece).start()

    def grad_copy(c):
        return pltpu.make_async_copy(
            grad_hbm.at[pl.ds(c * rows, rows)], feats.at[(layers - 1) % 2, c, t], io_sem.at[c]
        )

    def out_copy(c):
        return pltpu.make_async_copy(
            feats.at[1, c, t], out_hbm.at[pl.ds(c * rows, rows)], io_sem.at[c]
        )

    def project(level, c):
        out_factor[level, c] = lax.dot_general(
            proj_out[level], feats[level % 2, c, t], NT, preferred_element_type=f32
        )

    def finish(slot, level, c):
        for shift in range(1, n_tensor):
            feat_copy(level, c, shift).wait_send()
        total[c] = total[c] + part[slot, z].astype(f32)

        @pl.when(z > 0)
        def _():
            total[c] = total[c] + from_left[level % 2, c, last - z].astype(f32)

        @pl.when(z < last)
        def _():
            total[c] = total[c] + from_right[level % 2, c, z].astype(f32)

        feats[(level + 1) % 2, c, t] = total[c].astype(bf16)

        @pl.when(level > 0)
        def _():
            for shift in range(1, n_tensor):
                feat_copy(level - 1, c, shift).start()
            project(jnp.maximum(level - 1, 0), c)

        @pl.when(level == 0)
        def _():
            out_copy(c).start()

    def saved_copy(level):
        return pltpu.make_async_copy(saved_hbm.at[level], saved, load_sem.at[3])

    def share_of(i):
        return pl.ds(pl.multiple_of(i * share, share), share)

    def in_copy(shift):
        peer = lax.rem(t + shift, n_tensor)
        return pltpu.make_async_remote_copy(
            src_ref=in_mine.at[:, share_of(peer)],
            dst_ref=in_peer.at[shift - 1],
            send_sem=in_send_sem.at[shift - 1],
            recv_sem=in_recv_sem.at[shift - 1],
            device_id={"tensor": peer},
            device_id_type=MESH,
        )

    def run_copy(side):
        return pltpu.make_async_remote_copy(
            src_ref=run_send.at[side],
            dst_ref=run_recv.at[side],
            send_sem=run_send_sem.at[side],
            recv_sem=run_recv_sem.at[side],
            device_id={"layer": z + (1 if side == 0 else -1)},
            device_id_type=MESH,
        )

    def gather_copy(shift):
        return pltpu.make_async_remote_copy(
            src_ref=in_total.at[:, share_of(t)],
            dst_ref=in_total.at[:, share_of(t)],
            send_sem=gather_send_sem.at[shift - 1],
            recv_sem=gather_recv_sem.at[shift - 1],
            device_id={"tensor": lax.rem(t + shift, n_tensor)},
            device_id_type=MESH,
        )

    def owner_copy(shift):
        peer = lax.rem(z + shift, n_layer)
        return pltpu.make_async_remote_copy(
            src_ref=owner_send.at[peer],
            dst_ref=owner_recv.at[shift - 1],
            send_sem=owner_send_sem.at[shift - 1],
            recv_sem=owner_recv_sem.at[shift - 1],
            device_id={"layer": peer},
            device_id_type=MESH,
        )

    def tensor_copy(shift):
        return pltpu.make_async_remote_copy(
            src_ref=tensor_send,
            dst_ref=tensor_recv.at[shift - 1],
            send_sem=tensor_send_sem.at[shift - 1],
            recv_sem=tensor_recv_sem.at[shift - 1],
            device_id={"tensor": lax.rem(t + shift, n_tensor)},
            device_id_type=MESH,
        )

    def seq_copy(shift):
        return pltpu.make_async_remote_copy(
            src_ref=seq_blocks.at[0],
            dst_ref=seq_blocks.at[shift],
            send_sem=seq_send_sem.at[shift - 1],
            recv_sem=seq_recv_sem.at[shift - 1],
            device_id={"dp": lax.rem(d + shift, n_dp)},
            device_id_type=MESH,
        )

    def score_copy(shift):
        peer = lax.rem(z + shift, n_layer)
        return pltpu.make_async_remote_copy(
            src_ref=score_send.at[lax.rem(d - peer + n_dp, n_dp)],
            dst_ref=score_recv.at[shift - 1],
            send_sem=score_send_sem.at[shift - 1],
            recv_sem=score_recv_sem.at[shift - 1],
            device_id={"layer": peer},
            device_id_type=MESH,
        )

    def project_saved(level):
        saved_copy(level).wait()
        pair, half = level // 2, level % 2
        value = lax.dot_general(saved[...], proj_in[pair], NT, preferred_element_type=f32)
        if half == 0:
            in_mine[pair] = value.astype(bf16)
        else:
            lane = lax.broadcasted_iota(jnp.int32, value.shape, 1)
            in_mine[pair] = jnp.where(lane < rank, in_mine[pair].astype(f32), value).astype(bf16)
        if level + 1 < layers:
            saved_copy(level + 1).start()
        else:
            for shift in range(1, n_tensor):
                in_copy(shift).start()

    def run_step(s):
        if s == 0:
            value = in_mine[:, share_of(t)].astype(f32)
            for shift in range(1, n_tensor):
                in_copy(shift).wait()
                value = value + in_peer[shift - 1].astype(f32)
            in_sum[...] = value
        if s < last:

            @pl.when(z == s)
            def _():
                if s > 0:
                    run_copy(0).wait_recv()
                    run_send[0] = (in_sum[...] + run_recv[0].astype(f32)).astype(bf16)
                else:
                    run_send[0] = in_sum[...].astype(bf16)
                run_copy(0).start()

            @pl.when(z == last - s)
            def _():
                if s > 0:
                    run_copy(1).wait_recv()
                    run_send[1] = (in_sum[...] + run_recv[1].astype(f32)).astype(bf16)
                else:
                    run_send[1] = in_sum[...].astype(bf16)
                run_copy(1).start()

        else:

            @pl.when(z == last)
            def _():
                run_copy(0).wait_recv()

            @pl.when(z == 0)
            def _():
                run_copy(1).wait_recv()

            @pl.when(z < last)
            def _():
                run_copy(0).wait_send()
                in_sum[...] = in_sum[...] + run_recv[1].astype(f32)

            @pl.when(z > 0)
            def _():
                run_copy(1).wait_send()
                in_sum[...] = in_sum[...] + run_recv[0].astype(f32)

            in_total[:, share_of(t)] = in_sum[...].astype(bf16)
            for shift in range(1, n_tensor):
                gather_copy(shift).start()

    def send_blocks():
        for shift in range(1, n_tensor):
            gather_copy(shift).wait()
        lane = lax.broadcasted_iota(jnp.int32, (rank // 2, lanes), 1)
        for level in range(layers):
            pair, half = level // 2, level % 2
            acc = None
            for c in range(CHUNKS):
                term = lax.dot_general(
                    out_factor[level, c],
                    in_total[pair, c * rows : (c + 1) * rows].astype(f32),
                    NN,
                    precision=lax.Precision.HIGHEST,
                    preferred_element_type=f32,
                )
                acc = term if acc is None else acc + term
            block[...] = acc
            even = block[pl.ds(0, rank // 2, stride=2), :]
            odd = block[pl.ds(1, rank // 2, stride=2), :]
            if half == 0:
                odd = pltpu.roll(odd, rank, 1)
            else:
                even = pltpu.roll(even, rank, 1)
            level_blocks[level] = jnp.where(lane < rank, even, odd)
        for q in range(n_layer):
            level = jnp.int32(0)
            for k in range(1, layers):
                level = jnp.where(owner_ref[k] == q, k, level)
            owner_send[q] = level_blocks[level]
        for shift in range(1, n_layer):
            owner_copy(shift).start()

    def sum_layers():
        value = owner_send[z]
        for shift in range(1, n_layer):
            owner_copy(shift).wait()
            value = value + owner_recv[shift - 1]
        tensor_send[...] = value
        for shift in range(1, n_tensor):
            tensor_copy(shift).start()

    def sum_tensor():
        value = tensor_send[...]
        for shift in range(1, n_tensor):
            tensor_copy(shift).wait()
            value = value + tensor_recv[shift - 1]
        seq_blocks[0] = value
        for shift in range(1, n_dp):
            seq_copy(shift).start()

    def score():
        for shift in range(1, n_dp):
            seq_copy(shift).wait()
        pltpu.make_async_copy(query_hbm, queries, load_sem.at[2]).wait()
        acc = None
        for j in range(rank // 2):
            term = lax.dot_general(
                seq_blocks[:, j, :].astype(bf16),
                queries[:, j * lanes : (j + 1) * lanes],
                NT,
                preferred_element_type=f32,
            )
            acc = term if acc is None else acc + term
        for k in range(n_dp):
            score_send[k] = acc[k : k + 1]
        for shift in range(1, n_layer):
            score_copy(shift).start()

    def sum_scores():
        value = score_send[lax.rem(d - z + n_dp, n_dp)]
        for shift in range(1, n_layer):
            score_copy(shift).wait()
            value = value + score_recv[shift - 1]
        score_ref[...] = value

    barrier = pltpu.get_barrier_semaphore()
    for axis, size, here in (("tensor", n_tensor, t), ("layer", n_layer, z), ("dp", n_dp, d)):
        for shift in range(1, size):
            pl.semaphore_signal(
                barrier, inc=1, device_id={axis: lax.rem(here + shift, size)}, device_id_type=MESH
            )

    for c in range(CHUNKS):
        grad_copy(c).start()
    for n in range(RAW - 1):
        raw_copy(n).start()
    pltpu.make_async_copy(proj_out_hbm, proj_out, load_sem.at[0]).start()
    pltpu.make_async_copy(proj_in_hbm, proj_in, load_sem.at[1]).start()
    pl.semaphore_wait(barrier, n_tensor + n_layer + n_dp - 3)

    for c in range(CHUNKS):
        grad_copy(c).wait()
        for shift in range(1, n_tensor):
            feat_copy(layers - 1, c, shift).start()

    phases = layers * CHUNKS
    fraction = per_level // (2 * CHUNKS)

    @pl.loop(0, phases + 1)
    def _(p):
        level = layers - 1 - p // CHUNKS
        c = p % CHUNKS
        slot = p % 2
        old_level = layers - 1 - (p - 1) // CHUNKS
        old_c = (p + CHUNKS - 1) % CHUNKS
        old_slot = (p + 1) % 2

        def at_phase(k, task, *args):
            @pl.when(p == k)
            def _():
                task(*args)

        @pl.when(p > 0)
        def _():
            forward(old_slot, old_level, old_c, 1)

        @pl.when(p < phases)
        def _():
            @pl.when(p >= 2)
            def _():
                wait_part_sends(slot)

            @pl.loop(0, n_layer)
            def _(i):
                @pl.when(p == 0)
                def _():
                    relay(i * blocks, blocks)

                @pl.when(i == 0)
                def _():
                    for shift in range(1, n_tensor):
                        feat_copy(level, c, shift).wait_recv()

                multiply(slot, level, c, i)

        base = (layers - level) * per_level + c * 2 * fraction
        count = jnp.where(p == 1, 2 * fraction, fraction)

        @pl.when(p == 0)
        def _():
            pltpu.make_async_copy(proj_out_hbm, proj_out, load_sem.at[0]).wait()
            pltpu.make_async_copy(proj_in_hbm, proj_in, load_sem.at[1]).wait()
            pltpu.make_async_copy(query_hbm, queries, load_sem.at[2]).start()
            saved_copy(0).start()
            for k in range(CHUNKS):
                total[k] = feats[(layers - 1) % 2, k, t].astype(f32)
                project(layers - 1, k)

        at_phase(phases - 3, send_blocks)
        at_phase(phases - 1, sum_tensor)

        @pl.when((p > 0) & (level > 0) & (p < phases))
        def _():
            relay(jnp.where(p == 1, per_level, base), count)

        for s in range(2, n_layer - 1):

            @pl.when(p > 0)
            def _():
                forward(old_slot, old_level, old_c, s)

        for k in range(layers):
            at_phase(CHUNKS + k, project_saved, k)
        for k in range(n_layer):
            at_phase(CHUNKS + layers + k, run_step, k)
        at_phase(phases - 2, sum_layers)
        at_phase(phases - 1, score)

        @pl.when((p > 0) & (level > 0) & (p < phases))
        def _():
            relay(base + 2 * fraction - count, count)

        @pl.when(p > 0)
        def _():
            forward(old_slot, old_level, old_c, last)
            finish(old_slot, old_level, old_c)

    wait_part_sends((phases - 2) % 2)
    wait_part_sends((phases - 1) % 2)
    sum_scores()
    for c in range(CHUNKS):
        out_copy(c).wait()


def on_device(saved_inputs, output_grad, weights, proj_in, proj_out, query_grads, owner_map):
    weights = weights[:, :, :, 0, :]
    layers, in_rows, n_tensor, width = weights.shape
    tokens = output_grad.shape[0]
    rank = proj_out.shape[1]
    n_queries = query_grads.shape[1]
    n_layer, n_dp = lax.axis_size("layer"), lax.axis_size("dp")
    assert tokens == LEN and n_dp == n_layer == layers and layers % 2 == 0
    rows = tokens // CHUNKS
    piece_rows = in_rows // n_layer
    step = min(256, piece_rows // 2)
    pairs, lanes, share = layers // 2, 2 * rank, tokens // n_tensor
    bf16, f32 = jnp.bfloat16, jnp.float32
    dma = pltpu.SemaphoreType.DMA
    hops = n_layer - 1
    anywhere = pl.BlockSpec(memory_space=pl.ANY)
    return pl.pallas_call(
        functools.partial(
            stack_kernel, (layers, n_layer, n_tensor, n_dp, rows, width, rank, step)
        ),
        out_shape=(
            jax.ShapeDtypeStruct((tokens, width), bf16),
            jax.ShapeDtypeStruct((1, n_queries), f32),
        ),
        in_specs=[pl.BlockSpec(memory_space=pltpu.SMEM)] + [anywhere] * 6,
        out_specs=(anywhere, pl.BlockSpec(memory_space=pltpu.VMEM)),
        scratch_shapes=[
            pltpu.VMEM((RAW, step, n_tensor, width), bf16),
            pltpu.VMEM((2, n_layer, piece_rows, n_tensor * width), bf16),
            pltpu.VMEM((2, CHUNKS, n_tensor, rows, width), bf16),
            pltpu.VMEM((2, n_layer, rows, piece_rows), bf16),
            pltpu.VMEM((2, CHUNKS, hops, rows, piece_rows), bf16),
            pltpu.VMEM((2, CHUNKS, hops, rows, piece_rows), bf16),
            pltpu.VMEM((CHUNKS, rows, width), f32),
            pltpu.VMEM((pairs, lanes, width), bf16),
            pltpu.VMEM((layers, rank, width), bf16),
            pltpu.VMEM(query_grads.shape[1:], bf16),
            pltpu.VMEM((tokens, width), bf16),
            pltpu.VMEM((layers, CHUNKS, rank, rows), f32),
            pltpu.VMEM((pairs, tokens, lanes), bf16),
            pltpu.VMEM((n_tensor - 1, pairs, share, lanes), bf16),
            pltpu.VMEM((pairs, share, lanes), f32),
            pltpu.VMEM((2, pairs, share, lanes), bf16),
            pltpu.VMEM((2, pairs, share, lanes), bf16),
            pltpu.VMEM((pairs, tokens, lanes), bf16),
            pltpu.VMEM((rank, lanes), f32),
            pltpu.VMEM((layers, rank // 2, lanes), f32),
            pltpu.VMEM((n_layer, rank // 2, lanes), f32),
            pltpu.VMEM((hops, rank // 2, lanes), f32),
            pltpu.VMEM((rank // 2, lanes), f32),
            pltpu.VMEM((n_tensor - 1, rank // 2, lanes), f32),
            pltpu.VMEM((n_dp, rank // 2, lanes), f32),
            pltpu.VMEM((n_dp, 1, n_queries), f32),
            pltpu.VMEM((hops, 1, n_queries), f32),
            dma((RAW,)),
            dma((CHUNKS,)),
            dma((4,)),
            dma((2, CHUNKS, n_tensor - 1)),
            dma((2, CHUNKS, n_tensor - 1)),
            dma((2, n_layer)),
            dma((2, CHUNKS, hops)),
            dma((2, CHUNKS, hops)),
            dma((n_tensor - 1,)),
            dma((n_tensor - 1,)),
            dma((2,)),
            dma((2,)),
            dma((n_tensor - 1,)),
            dma((n_tensor - 1,)),
            dma((hops,)),
            dma((hops,)),
            dma((n_tensor - 1,)),
            dma((n_tensor - 1,)),
            dma((n_dp - 1,)),
            dma((n_dp - 1,)),
            dma((hops,)),
            dma((hops,)),
        ],
        compiler_params=pltpu.CompilerParams(
            collective_id=0, has_side_effects=True, vmem_limit_bytes=VMEM_BYTES
        ),
        name="backward_stack",
    )(
        owner_map,
        output_grad,
        weights,
        saved_inputs,
        proj_in.reshape(pairs, lanes, width),
        proj_out,
        query_grads[0],
    )


def solution(mesh):
    in_specs = (
        P(None, "dp", ("tensor", "layer")),
        P("dp", ("tensor", "layer")),
        P(None, "tensor", None, "layer", None),
        P(None, None, ("tensor", "layer")),
        P(None, None, ("tensor", "layer")),
        P("layer", ("dp", "tensor"), None),
        P(),
    )
    out_specs = (P("dp", ("tensor", "layer")), P("layer", ("dp", "tensor")))
    return jax.shard_map(
        on_device, mesh=mesh, in_specs=in_specs, out_specs=out_specs, check_vma=False
    )
```

time: 434 us -> 339 us (0.78)
  waiting for transfers between devices: 61.6 us -> 0 us
  blocking collectives: 25 us -> 0 us
  Pallas kernels: 320 us -> 335 us
  between operations: 14.1 us -> 0.64 us
  matrix products: 5.4 us -> 0 us
    reduce_scatter x1 -> x0, waiting for transfers between devices: 61.6 us -> none  [on_device(): lax.psum_scatter(ordered, ('tensor', 'layer'), scatter_dimension=0, tiled...]
    psum x2 -> x0, blocking collectives: 19.7 us -> none  [the longest x1 10.3 us: on_device(): total = lax.psum(partial_scores, 'layer')]
    pallas_call x1, Pallas kernels: 320 us -> 335 us  [on_device(): pl.pallas_call(functools.partial(stack_kernel, (layers, n_layer, n_tensor...]
    dot_general x3 -> x0, matrix products: 5.4 us -> none  [the longest x1 3.78 us: on_device(): jnp.einsum('ltd,lrd->ltr', saved_inputs, proj_in, preferred_element_type=...]
    all_gather x1 -> x0, blocking collectives: 5.24 us -> none  [on_device(): lax.all_gather(blocks_bf, 'dp', axis=0, tiled=True)]
  transfers between devices with their start and end apart: 1 -> 0, of which waited for: 1 -> 0; matrix products, arithmetic and copies ran while one was open for 0% -> 0% of each run, Pallas kernels for 0% -> 0%
where the time goes in v1:
time: 339 us
  Pallas kernels  335 us (99%)
    pallas_call x1, Pallas kernels, on_device(): pl.pallas_call(functools.partial(stack_kernel, (layers, n_layer, n_tensor...  335 us

profile of v1, /device:TPU:0, one launch (start us, length us, event | category | flops | bytes accessed | tf_op | source)
XLA Modules:
  0.0 338.6 jit_solution(14820846017206902346)
XLA Ops:
  0.6 334.6 %backward_stack.1 = (bf16[512,1024]{1,0:T(8,128)(2,1)}, f32[1,128]{1,0:T(1,128)}) custom-call(s32[4]{0:T(128)} %owner_ref.1, bf16[512,1024]{1,0:T(8,128)(2,1)} %grad_hbm.1, bf16[4,4096,2,1024]{3,2,1,0:T(2,128)(2,1)} %bitcast.weight_hbm, bf16[4,512,1024]{2,1,0:T(8,128)(2,1)} %saved_hbm.1, bf16[2,128,1024]{2,1,0:T(8,128)(2,1)} %bitcast.4, ...), custom_call_target="tpu_custom_call" | custom-call | tf_op jit(solution)/shard_map/backward_stack/pallas_call | solution.py:602
  335.2 2.3 copy.11
  337.5 1.1 copy.12

commit v2 on v1

--- a/solution.py
+++ b/solution.py
@@ -114,13 +114,17 @@
             level = layers - 1 - n // per_level
             q = nth_piece((n // blocks) % n_layer)
             at = pl.ds(pl.multiple_of((n % blocks) * step, step), step)
+            by_feature = jnp.swapaxes(raw[n % RAW], 0, 1)
             for a in range(n_tensor):
-                flat[level % 2, q, at, a * width : (a + 1) * width] = raw[n % RAW, :, a, :]
+                flat[level % 2, q, at, a * width : (a + 1) * width] = by_feature[a]
+
+    def span(c, count=1):
+        return pl.ds(pl.multiple_of(c * rows, rows), count * rows)
 
     def feat_copy(level, c, shift):
         return pltpu.make_async_remote_copy(
-            src_ref=feats.at[level % 2, c, t],
-            dst_ref=feats.at[level % 2, c, t],
+            src_ref=feats.at[level % 2, t, span(c)],
+            dst_ref=feats.at[level % 2, t, span(c)],
             send_sem=feat_send.at[level % 2, c, shift - 1],
             recv_sem=feat_recv.at[level % 2, c, shift - 1],
             device_id={"tensor": lax.rem(t + shift, n_tensor)},
@@ -129,9 +133,9 @@
 
     def right_copy(slot, level, c, q):
         return pltpu.make_async_remote_copy(
-            src_ref=part.at[slot, q],
+            src_ref=part.at[slot, q, span(c % 2)],
             dst_ref=from_left.at[level % 2, c, last - q],
-            send_sem=part_send.at[slot, q],
+            send_sem=part_send.at[slot, c % 2, q],
             recv_sem=left_recv.at[level % 2, c, last - q],
             device_id={"layer": z + 1},
             device_id_type=MESH,
@@ -139,31 +143,41 @@
 
     def left_copy(slot, level, c, q):
         return pltpu.make_async_remote_copy(
-            src_ref=part.at[slot, q],
+            src_ref=part.at[slot, q, span(c % 2)],
             dst_ref=from_right.at[level % 2, c, q],
-            send_sem=part_send.at[slot, q],
+            send_sem=part_send.at[slot, c % 2, q],
             recv_sem=right_recv.at[level % 2, c, q],
             device_id={"layer": z - 1},
             device_id_type=MESH,
         )
 
-    def wait_part_sends(slot):
+    def wait_part_sends(slot, half):
         for q in range(n_layer):
 
             if q > 0:
 
                 @pl.when(q > z)
                 def _():
-                    right_copy(slot, 0, 0, q).wait_send()
+                    right_copy(slot, 0, half, q).wait_send()
 
             if q < last:
 
                 @pl.when(q < z)
                 def _():
-                    left_copy(slot, 0, 0, q).wait_send()
-
-    def multiply(slot, level, c, i):
+                    left_copy(slot, 0, half, q).wait_send()
+
+    def send_piece(slot, level, c, q):
+        @pl.when((z == 0) & (q > 0))
+        def _():
+            right_copy(slot, level, c, q).start()
+
+        @pl.when((z == last) & (q < last))
+        def _():
+            left_copy(slot, level, c, q).start()
+
+    def multiply(slot, level, c, i, count):
         q = nth_piece(i)
+        here, there = span(c, count), span(c % 2, count)
 
         @pl.loop(0, piece_rows // n_tile)
         def _(j):
@@ -171,21 +185,15 @@
             acc = None
             for a in range(n_tensor):
                 term = lax.dot_general(
-                    feats[level % 2, c, a],
+                    feats[level % 2, a, here, :],
                     flat[level % 2, q, at, a * width : (a + 1) * width],
                     NT,
                     preferred_element_type=f32,
                 )
                 acc = term if acc is None else acc + term
-            part[slot, q, :, at] = acc.astype(bf16)
-
-        @pl.when((z == 0) & (q > 0))
-        def _():
-            right_copy(slot, level, c, q).start()
-
-        @pl.when((z == last) & (q < last))
-        def _():
-            left_copy(slot, level, c, q).start()
+            part[slot, q, there, at] = acc.astype(bf16)
+
+        send_piece(slot, level, c, q)
 
     def forward(slot, level, c, s):
         right_piece, left_piece = last - s + z, s - last + z
@@ -196,8 +204,8 @@
 
             @pl.when(right_piece > z)
             def _():
-                part[slot, right_piece] = (
-                    part[slot, right_piece].astype(f32)
+                part[slot, right_piece, span(c % 2), :] = (
+                    part[slot, right_piece, span(c % 2), :].astype(f32)
                     + from_left[level % 2, c, last - right_piece].astype(f32)
                 ).astype(bf16)
                 right_copy(slot, level, c, right_piece).start()
@@ -208,31 +216,31 @@
 
             @pl.when(left_piece < z)
             def _():
-                part[slot, left_piece] = (
-                    part[slot, left_piece].astype(f32)
+                part[slot, left_piece, span(c % 2), :] = (
+                    part[slot, left_piece, span(c % 2), :].astype(f32)
                     + from_right[level % 2, c, left_piece].astype(f32)
                 ).astype(bf16)
                 left_copy(slot, level, c, left_piece).start()
 
     def grad_copy(c):
         return pltpu.make_async_copy(
-            grad_hbm.at[pl.ds(c * rows, rows)], feats.at[(layers - 1) % 2, c, t], io_sem.at[c]
+            grad_hbm.at[pl.ds(c * rows, rows)], feats.at[(layers - 1) % 2, t, span(c)], io_sem.at[c]
         )
 
     def out_copy(c):
         return pltpu.make_async_copy(
-            feats.at[1, c, t], out_hbm.at[pl.ds(c * rows, rows)], io_sem.at[c]
+            feats.at[1, t, span(c)], out_hbm.at[pl.ds(c * rows, rows)], io_sem.at[c]
         )
 
     def project(level, c):
         out_factor[level, c] = lax.dot_general(
-            proj_out[level], feats[level % 2, c, t], NT, preferred_element_type=f32
+            proj_out[level], feats[level % 2, t, span(c), :], NT, preferred_element_type=f32
         )
 
     def finish(slot, level, c):
         for shift in range(1, n_tensor):
             feat_copy(level, c, shift).wait_send()
-        total[c] = total[c] + part[slot, z].astype(f32)
+        total[c] = total[c] + part[slot, z, span(c % 2), :].astype(f32)
 
         @pl.when(z > 0)
         def _():
@@ -242,7 +250,7 @@
         def _():
             total[c] = total[c] + from_right[level % 2, c, z].astype(f32)
 
-        feats[(level + 1) % 2, c, t] = total[c].astype(bf16)
+        feats[(level + 1) % 2, t, span(c), :] = total[c].astype(bf16)
 
         @pl.when(level > 0)
         def _():
@@ -501,10 +509,10 @@
     def _(p):
         level = layers - 1 - p // CHUNKS
         c = p % CHUNKS
-        slot = p % 2
+        slot = (p // 2) % 2
         old_level = layers - 1 - (p - 1) // CHUNKS
         old_c = (p + CHUNKS - 1) % CHUNKS
-        old_slot = (p + 1) % 2
+        old_slot = ((p - 1) // 2) % 2
 
         def at_phase(k, task, *args):
             @pl.when(p == k)
@@ -515,12 +523,8 @@
         def _():
             forward(old_slot, old_level, old_c, 1)
 
-        @pl.when(p < phases)
-        def _():
-            @pl.when(p >= 2)
-            def _():
-                wait_part_sends(slot)
-
+        @pl.when(p < 2)
+        def _():
             @pl.loop(0, n_layer)
             def _(i):
                 @pl.when(p == 0)
@@ -532,11 +536,29 @@
                     for shift in range(1, n_tensor):
                         feat_copy(level, c, shift).wait_recv()
 
-                multiply(slot, level, c, i)
+                multiply(slot, level, c, i, 1)
+
+        @pl.when((p >= 2) & (p < phases) & (c % 2 == 0))
+        def _():
+            @pl.when(p >= 4)
+            def _():
+                wait_part_sends(slot, 0)
+                wait_part_sends(slot, 1)
+
+            for shift in range(1, n_tensor):
+                feat_copy(level, c, shift).wait_recv()
+                feat_copy(level, c + 1, shift).wait_recv()
+
+            @pl.loop(0, n_layer)
+            def _(i):
+                multiply(slot, level, c, i, 2)
+
+            for i in range(n_layer):
+                send_piece(slot, level, c + 1, nth_piece(i))
 
         base = (layers - level) * per_level + c * 2 * fraction
-        count = jnp.where(p == 1, 2 * fraction, fraction)
-
+        early = jnp.where(p == 1, 2 * fraction, jnp.where(c % 2 == 1, fraction, 0))
+        late = jnp.where((p == 1) | (c % 2 == 0), 2 * fraction, fraction)
         @pl.when(p == 0)
         def _():
             pltpu.make_async_copy(proj_out_hbm, proj_out, load_sem.at[0]).wait()
@@ -544,7 +566,7 @@
             pltpu.make_async_copy(query_hbm, queries, load_sem.at[2]).start()
             saved_copy(0).start()
             for k in range(CHUNKS):
-                total[k] = feats[(layers - 1) % 2, k, t].astype(f32)
+                total[k] = feats[(layers - 1) % 2, t, span(k), :].astype(f32)
                 project(layers - 1, k)
 
         at_phase(phases - 3, send_blocks)
@@ -552,7 +574,7 @@
 
         @pl.when((p > 0) & (level > 0) & (p < phases))
         def _():
-            relay(jnp.where(p == 1, per_level, base), count)
+            relay(jnp.where(p == 1, per_level, base), early)
 
         for s in range(2, n_layer - 1):
 
@@ -569,15 +591,16 @@
 
         @pl.when((p > 0) & (level > 0) & (p < phases))
         def _():
-            relay(base + 2 * fraction - count, count)
+            relay(base + 2 * fraction - late, late)
 
         @pl.when(p > 0)
         def _():
             forward(old_slot, old_level, old_c, last)
             finish(old_slot, old_level, old_c)
 
-    wait_part_sends((phases - 2) % 2)
-    wait_part_sends((phases - 1) % 2)
+    for k in range(2):
+        wait_part_sends(k, 0)
+        wait_part_sends(k, 1)
     sum_scores()
     for c in range(CHUNKS):
         out_copy(c).wait()
@@ -612,8 +635,8 @@
         scratch_shapes=[
             pltpu.VMEM((RAW, step, n_tensor, width), bf16),
             pltpu.VMEM((2, n_layer, piece_rows, n_tensor * width), bf16),
-            pltpu.VMEM((2, CHUNKS, n_tensor, rows, width), bf16),
-            pltpu.VMEM((2, n_layer, rows, piece_rows), bf16),
+            pltpu.VMEM((2, n_tensor, tokens, width), bf16),
+            pltpu.VMEM((2, n_layer, 2 * rows, piece_rows), bf16),
             pltpu.VMEM((2, CHUNKS, hops, rows, piece_rows), bf16),
             pltpu.VMEM((2, CHUNKS, hops, rows, piece_rows), bf16),
             pltpu.VMEM((CHUNKS, rows, width), f32),
@@ -642,7 +665,7 @@
             dma((4,)),
             dma((2, CHUNKS, n_tensor - 1)),
             dma((2, CHUNKS, n_tensor - 1)),
-            dma((2, n_layer)),
+            dma((2, 2, n_layer)),
             dma((2, CHUNKS, hops)),
             dma((2, CHUNKS, hops)),
             dma((n_tensor - 1,)),

time: 339 us -> 300 us (0.88)
  Pallas kernels: 335 us -> 295 us
    pallas_call x1, Pallas kernels: 335 us -> 295 us  [on_device(): pl.pallas_call(functools.partial(stack_kernel, (layers, n_layer, n_tensor...]
where the time goes in v2:
time: 300 us; the launch traced here: 299 us
  Pallas kernels  295 us (98%)
  local copies, waits for them, and re-layouts  3.38 us (1%)
    pallas_call x1, Pallas kernels, on_device(): pl.pallas_call(functools.partial(stack_kernel, (layers, n_layer, n_tensor...  295 us

profile of v2, /device:TPU:0, one launch (start us, length us, event | category | flops | bytes accessed | tf_op | source)
XLA Modules:
  0.0 299.0 jit_solution(7030181142543056129)
XLA Ops:
  0.6 295.0 %backward_stack.1 = (bf16[512,1024]{1,0:T(8,128)(2,1)}, f32[1,128]{1,0:T(1,128)}) custom-call(s32[4]{0:T(128)} %owner_ref.1, bf16[512,1024]{1,0:T(8,128)(2,1)} %grad_hbm.1, bf16[4,4096,2,1024]{3,2,1,0:T(2,128)(2,1)} %bitcast.weight_hbm, bf16[4,512,1024]{2,1,0:T(8,128)(2,1)} %saved_hbm.1, bf16[2,128,1024]{2,1,0:T(8,128)(2,1)} %bitcast.4, ...), custom_call_target="tpu_custom_call" | custom-call | tf_op jit(solution)/shard_map/backward_stack/pallas_call | solution.py:625
  295.6 2.3 copy.11
  297.9 1.1 copy.12

commit v3 on v2

--- a/solution.py
+++ b/solution.py
@@ -59,6 +59,7 @@
     load_sem,
     feat_send,
     feat_recv,
+    first_recv,
     part_send,
     left_recv,
     right_recv,
@@ -87,6 +88,7 @@
     tokens = rows * CHUNKS
     share = tokens // n_tensor
     lanes = 2 * rank
+    first_rows = rows // 2
     z = lax.axis_index("layer")
     t = lax.axis_index("tensor")
     d = lax.axis_index("dp")
@@ -131,20 +133,31 @@
             device_id_type=MESH,
         )
 
-    def right_copy(slot, level, c, q):
-        return pltpu.make_async_remote_copy(
-            src_ref=part.at[slot, q, span(c % 2)],
-            dst_ref=from_left.at[level % 2, c, last - q],
+    def first_copy(half, shift):
+        here = slice(half * first_rows, (half + 1) * first_rows)
+        return pltpu.make_async_remote_copy(
+            src_ref=feats.at[(layers - 1) % 2, t, here],
+            dst_ref=feats.at[(layers - 1) % 2, t, here],
+            send_sem=feat_send.at[(layers - 1) % 2, 0, shift - 1],
+            recv_sem=first_recv.at[half, shift - 1],
+            device_id={"tensor": lax.rem(t + shift, n_tensor)},
+            device_id_type=MESH,
+        )
+
+    def right_copy(slot, level, c, q, first=0, count=rows):
+        return pltpu.make_async_remote_copy(
+            src_ref=part.at[slot, q, pl.ds(pl.multiple_of((c % 2) * rows + first, count), count)],
+            dst_ref=from_left.at[level % 2, c, last - q, first : first + count],
             send_sem=part_send.at[slot, c % 2, q],
             recv_sem=left_recv.at[level % 2, c, last - q],
             device_id={"layer": z + 1},
             device_id_type=MESH,
         )
 
-    def left_copy(slot, level, c, q):
-        return pltpu.make_async_remote_copy(
-            src_ref=part.at[slot, q, span(c % 2)],
-            dst_ref=from_right.at[level % 2, c, q],
+    def left_copy(slot, level, c, q, first=0, count=rows):
+        return pltpu.make_async_remote_copy(
+            src_ref=part.at[slot, q, pl.ds(pl.multiple_of((c % 2) * rows + first, count), count)],
+            dst_ref=from_right.at[level % 2, c, q, first : first + count],
             send_sem=part_send.at[slot, c % 2, q],
             recv_sem=right_recv.at[level % 2, c, q],
             device_id={"layer": z - 1},
@@ -166,19 +179,16 @@
                 def _():
                     left_copy(slot, 0, half, q).wait_send()
 
-    def send_piece(slot, level, c, q):
+    def send_piece(slot, level, c, q, *part_rows):
         @pl.when((z == 0) & (q > 0))
         def _():
-            right_copy(slot, level, c, q).start()
+            right_copy(slot, level, c, q, *part_rows).start()
 
         @pl.when((z == last) & (q < last))
         def _():
-            left_copy(slot, level, c, q).start()
-
-    def multiply(slot, level, c, i, count):
-        q = nth_piece(i)
-        here, there = span(c, count), span(c % 2, count)
-
+            left_copy(slot, level, c, q, *part_rows).start()
+
+    def multiply(slot, level, q, here, there):
         @pl.loop(0, piece_rows // n_tile)
         def _(j):
             at = pl.ds(pl.multiple_of(j * n_tile, n_tile), n_tile)
@@ -192,8 +202,6 @@
                 )
                 acc = term if acc is None else acc + term
             part[slot, q, there, at] = acc.astype(bf16)
-
-        send_piece(slot, level, c, q)
 
     def forward(slot, level, c, s):
         right_piece, left_piece = last - s + z, s - last + z
@@ -483,7 +491,16 @@
         score_ref[...] = value
 
     barrier = pltpu.get_barrier_semaphore()
-    for axis, size, here in (("tensor", n_tensor, t), ("layer", n_layer, z), ("dp", n_dp, d)):
+
+    @pl.when(z > 0)
+    def _():
+        pl.semaphore_signal(barrier, inc=1, device_id={"layer": z - 1}, device_id_type=MESH)
+
+    @pl.when(z < last)
+    def _():
+        pl.semaphore_signal(barrier, inc=1, device_id={"layer": z + 1}, device_id_type=MESH)
+
+    for axis, size, here in (("tensor", n_tensor, t), ("dp", n_dp, d)):
         for shift in range(1, size):
             pl.semaphore_signal(
                 barrier, inc=1, device_id={axis: lax.rem(here + shift, size)}, device_id_type=MESH
@@ -495,17 +512,23 @@
         raw_copy(n).start()
     pltpu.make_async_copy(proj_out_hbm, proj_out, load_sem.at[0]).start()
     pltpu.make_async_copy(proj_in_hbm, proj_in, load_sem.at[1]).start()
-    pl.semaphore_wait(barrier, n_tensor + n_layer + n_dp - 3)
+    pl.semaphore_wait(
+        barrier, n_tensor + n_dp - 2 + jnp.minimum(z, 1) + jnp.minimum(last - z, 1)
+    )
 
     for c in range(CHUNKS):
         grad_copy(c).wait()
         for shift in range(1, n_tensor):
-            feat_copy(layers - 1, c, shift).start()
+            if c == 0:
+                first_copy(0, shift).start()
+                first_copy(1, shift).start()
+            else:
+                feat_copy(layers - 1, c, shift).start()
 
     phases = layers * CHUNKS
     fraction = per_level // (2 * CHUNKS)
 
-    @pl.loop(0, phases + 1)
+    @pl.loop(0, phases - 1)
     def _(p):
         level = layers - 1 - p // CHUNKS
         c = p % CHUNKS
@@ -523,22 +546,34 @@
         def _():
             forward(old_slot, old_level, old_c, 1)
 
-        @pl.when(p < 2)
-        def _():
+        @pl.when(p == 0)
+        def _():
+            relay(0, blocks)
+            q = nth_piece(0)
+            for half in range(2):
+                first = half * first_rows
+                for shift in range(1, n_tensor):
+                    first_copy(half, shift).wait_recv()
+                multiply(slot, level, q, pl.ds(first, first_rows), pl.ds(first, first_rows))
+                send_piece(slot, level, 0, q, first, first_rows)
+
+            @pl.loop(1, n_layer)
+            def _(i):
+                relay(i * blocks, blocks)
+                multiply(slot, level, nth_piece(i), pl.ds(0, rows), pl.ds(0, rows))
+                send_piece(slot, level, 0, nth_piece(i))
+
+        @pl.when(p == 1)
+        def _():
+            for shift in range(1, n_tensor):
+                feat_copy(level, 1, shift).wait_recv()
+
             @pl.loop(0, n_layer)
             def _(i):
-                @pl.when(p == 0)
-                def _():
-                    relay(i * blocks, blocks)
-
-                @pl.when(i == 0)
-                def _():
-                    for shift in range(1, n_tensor):
-                        feat_copy(level, c, shift).wait_recv()
-
-                multiply(slot, level, c, i, 1)
-
-        @pl.when((p >= 2) & (p < phases) & (c % 2 == 0))
+                multiply(slot, level, nth_piece(i), pl.ds(rows, rows), pl.ds(rows, rows))
+                send_piece(slot, level, 1, nth_piece(i))
+
+        @pl.when((p >= 2) & (c % 2 == 0))
         def _():
             @pl.when(p >= 4)
             def _():
@@ -551,10 +586,18 @@
 
             @pl.loop(0, n_layer)
             def _(i):
-                multiply(slot, level, c, i, 2)
-
-            for i in range(n_layer):
-                send_piece(slot, level, c + 1, nth_piece(i))
+                q = nth_piece(i)
+                multiply(slot, level, q, span(c, 2), pl.ds(0, 2 * rows))
+                send_piece(slot, level, c, q)
+
+                @pl.when(p == phases - 2)
+                def _():
+                    send_piece(slot, level, c + 1, q)
+
+            @pl.when(p < phases - 2)
+            def _():
+                for i in range(n_layer):
+                    send_piece(slot, level, c + 1, nth_piece(i))
 
         base = (layers - level) * per_level + c * 2 * fraction
         early = jnp.where(p == 1, 2 * fraction, jnp.where(c % 2 == 1, fraction, 0))
@@ -570,9 +613,8 @@
                 project(layers - 1, k)
 
         at_phase(phases - 3, send_blocks)
-        at_phase(phases - 1, sum_tensor)
-
-        @pl.when((p > 0) & (level > 0) & (p < phases))
+
+        @pl.when((p > 0) & (level > 0))
         def _():
             relay(jnp.where(p == 1, per_level, base), early)
 
@@ -587,9 +629,8 @@
         for k in range(n_layer):
             at_phase(CHUNKS + layers + k, run_step, k)
         at_phase(phases - 2, sum_layers)
-        at_phase(phases - 1, score)
-
-        @pl.when((p > 0) & (level > 0) & (p < phases))
+
+        @pl.when((p > 0) & (level > 0))
         def _():
             relay(base + 2 * fraction - late, late)
 
@@ -598,10 +639,21 @@
             forward(old_slot, old_level, old_c, last)
             finish(old_slot, old_level, old_c)
 
+    end_slot, end_level = ((phases - 1) // 2) % 2, jnp.int32(0)
+    pair = (CHUNKS - 2, CHUNKS - 1)
+    for s in range(1, last):
+        for c in pair:
+            forward(end_slot, end_level, c, s)
+        if s == 1:
+            sum_tensor()
+    score()
+    for c in pair:
+        forward(end_slot, end_level, c, last)
+        finish(end_slot, end_level, c)
+    sum_scores()
     for k in range(2):
         wait_part_sends(k, 0)
         wait_part_sends(k, 1)
-    sum_scores()
     for c in range(CHUNKS):
         out_copy(c).wait()
 
@@ -665,6 +717,7 @@
             dma((4,)),
             dma((2, CHUNKS, n_tensor - 1)),
             dma((2, CHUNKS, n_tensor - 1)),
+            dma((2, n_tensor - 1)),
             dma((2, 2, n_layer)),
             dma((2, CHUNKS, hops)),
             dma((2, CHUNKS, hops)),

time: 300 us -> 295 us (0.983)
  Pallas kernels: 295 us -> 290 us
    pallas_call x1, Pallas kernels: 295 us -> 290 us  [on_device(): pl.pallas_call(functools.partial(stack_kernel, (layers, n_layer, n_tensor...]
where the time goes in v3:
time: 295 us; the launch traced here: 294 us
  Pallas kernels  290 us (98%)
  local copies, waits for them, and re-layouts  3.38 us (1%)
    pallas_call x1, Pallas kernels, on_device(): pl.pallas_call(functools.partial(stack_kernel, (layers, n_layer, n_tensor...  290 us

profile of v3, /device:TPU:0, one launch (start us, length us, event | category | flops | bytes accessed | tf_op | source)
XLA Modules:
  0.0 294.4 jit_solution(4066413380113894153)
XLA Ops:
  0.6 290.4 %backward_stack.1 = (bf16[512,1024]{1,0:T(8,128)(2,1)}, f32[1,128]{1,0:T(1,128)}) custom-call(s32[4]{0:T(128)} %owner_ref.1, bf16[512,1024]{1,0:T(8,128)(2,1)} %grad_hbm.1, bf16[4,4096,2,1024]{3,2,1,0:T(2,128)(2,1)} %bitcast.weight_hbm, bf16[4,512,1024]{2,1,0:T(8,128)(2,1)} %saved_hbm.1, bf16[2,128,1024]{2,1,0:T(8,128)(2,1)} %bitcast.4, ...), custom_call_target="tpu_custom_call" | custom-call | tf_op jit(solution)/shard_map/backward_stack/pallas_call | solution.py:677
  291.0 2.3 copy.11
  293.3 1.1 copy.12

commit v4 on v3

--- a/solution.py
+++ b/solution.py
@@ -10,6 +10,7 @@
 LEN = 512
 CHUNKS = 4
 RAW = 3
+FIRST = 4
 MESH = pl.DeviceIdType.MESH
 VMEM_BYTES = 67_000_000
 NT = (((1,), (1,)), ((), ()))
@@ -26,9 +27,10 @@
     proj_out_hbm,
     query_hbm,
     out_hbm,
-    score_ref,
+    score_hbm,
     raw,
     flat,
+    ahead,
     feats,
     part,
     from_left,
@@ -54,6 +56,7 @@
     seq_blocks,
     score_send,
     score_recv,
+    score_total,
     raw_sem,
     io_sem,
     load_sem,
@@ -88,7 +91,7 @@
     tokens = rows * CHUNKS
     share = tokens // n_tensor
     lanes = 2 * rank
-    first_rows = rows // 2
+    first_rows = rows // FIRST
     z = lax.axis_index("layer")
     t = lax.axis_index("tensor")
     d = lax.axis_index("dp")
@@ -202,6 +205,41 @@
                 )
                 acc = term if acc is None else acc + term
             part[slot, q, there, at] = acc.astype(bf16)
+
+    def start_piece(slot, level, q):
+        def features_of(a):
+            return pl.ds(pl.multiple_of(a * width, width), width)
+
+        @pl.loop(0, piece_rows // n_tile)
+        def _(j):
+            at = pl.ds(pl.multiple_of(j * n_tile, n_tile), n_tile)
+            ahead[:, at] = lax.dot_general(
+                feats[level % 2, t, 0:rows, :],
+                flat[level % 2, q, at, features_of(t)],
+                NT,
+                preferred_element_type=f32,
+            )
+
+        for k in range(FIRST):
+            here = slice(k * first_rows, (k + 1) * first_rows)
+            for shift in range(1, n_tensor):
+                first_copy(k, shift).wait_recv()
+
+            @pl.loop(0, piece_rows // n_tile)
+            def _(j):
+                at = pl.ds(pl.multiple_of(j * n_tile, n_tile), n_tile)
+                acc = ahead[here, at]
+                for shift in range(1, n_tensor):
+                    a = lax.rem(t + shift, n_tensor)
+                    acc = acc + lax.dot_general(
+                        feats[level % 2, a, here, :],
+                        flat[level % 2, q, at, features_of(a)],
+                        NT,
+                        preferred_element_type=f32,
+                    )
+                part[slot, q, here, at] = acc.astype(bf16)
+
+            send_piece(slot, level, 0, q, k * first_rows, first_rows)
 
     def forward(slot, level, c, s):
         right_piece, left_piece = last - s + z, s - last + z
@@ -483,12 +521,16 @@
         for shift in range(1, n_layer):
             score_copy(shift).start()
 
+    def score_out():
+        return pltpu.make_async_copy(score_total, score_hbm, load_sem.at[4])
+
     def sum_scores():
         value = score_send[lax.rem(d - z + n_dp, n_dp)]
         for shift in range(1, n_layer):
             score_copy(shift).wait()
             value = value + score_recv[shift - 1]
-        score_ref[...] = value
+        score_total[...] = value
+        score_out().start()
 
     barrier = pltpu.get_barrier_semaphore()
 
@@ -520,8 +562,8 @@
         grad_copy(c).wait()
         for shift in range(1, n_tensor):
             if c == 0:
-                first_copy(0, shift).start()
-                first_copy(1, shift).start()
+                for k in range(FIRST):
+                    first_copy(k, shift).start()
             else:
                 feat_copy(layers - 1, c, shift).start()
 
@@ -549,13 +591,7 @@
         @pl.when(p == 0)
         def _():
             relay(0, blocks)
-            q = nth_piece(0)
-            for half in range(2):
-                first = half * first_rows
-                for shift in range(1, n_tensor):
-                    first_copy(half, shift).wait_recv()
-                multiply(slot, level, q, pl.ds(first, first_rows), pl.ds(first, first_rows))
-                send_piece(slot, level, 0, q, first, first_rows)
+            start_piece(slot, level, nth_piece(0))
 
             @pl.loop(1, n_layer)
             def _(i):
@@ -654,8 +690,48 @@
     for k in range(2):
         wait_part_sends(k, 0)
         wait_part_sends(k, 1)
+    score_out().wait()
     for c in range(CHUNKS):
         out_copy(c).wait()
+
+
+def hand_over_kernel(grad_in, score_in, grad_out, score_out, grad, score, in_sem, out_sem):
+    count = in_sem.shape[0] - 1
+    rows = grad.shape[0] // count
+
+    def copies(source, target, sem):
+        for k in range(count):
+            at = pl.ds(k * rows, rows)
+            yield pltpu.make_async_copy(source[0].at[at], target[0].at[at], sem.at[k])
+        yield pltpu.make_async_copy(source[1], target[1], sem.at[count])
+
+    loads = list(copies((grad_in, score_in), (grad, score), in_sem))
+    stores = list(copies((grad, score), (grad_out, score_out), out_sem))
+    for load in loads:
+        load.start()
+    for load, store in zip(loads, stores):
+        load.wait()
+        store.start()
+    for store in stores:
+        store.wait()
+
+
+def hand_over(grad, score):
+    shapes = tuple(jax.ShapeDtypeStruct(x.shape, x.dtype) for x in (grad, score))
+    anywhere = pl.BlockSpec(memory_space=pl.ANY)
+    return pl.pallas_call(
+        hand_over_kernel,
+        out_shape=shapes,
+        in_specs=[anywhere] * 2,
+        out_specs=(anywhere,) * 2,
+        scratch_shapes=[
+            pltpu.VMEM(grad.shape, grad.dtype),
+            pltpu.VMEM(score.shape, score.dtype),
+            pltpu.SemaphoreType.DMA((CHUNKS + 1,)),
+            pltpu.SemaphoreType.DMA((CHUNKS + 1,)),
+        ],
+        name="hand_over",
+    )(grad, score)
 
 
 def on_device(saved_inputs, output_grad, weights, proj_in, proj_out, query_grads, owner_map):
@@ -674,7 +750,7 @@
     dma = pltpu.SemaphoreType.DMA
     hops = n_layer - 1
     anywhere = pl.BlockSpec(memory_space=pl.ANY)
-    return pl.pallas_call(
+    results = pl.pallas_call(
         functools.partial(
             stack_kernel, (layers, n_layer, n_tensor, n_dp, rows, width, rank, step)
         ),
@@ -683,10 +759,11 @@
             jax.ShapeDtypeStruct((1, n_queries), f32),
         ),
         in_specs=[pl.BlockSpec(memory_space=pltpu.SMEM)] + [anywhere] * 6,
-        out_specs=(anywhere, pl.BlockSpec(memory_space=pltpu.VMEM)),
+        out_specs=(anywhere, anywhere),
         scratch_shapes=[
             pltpu.VMEM((RAW, step, n_tensor, width), bf16),
             pltpu.VMEM((2, n_layer, piece_rows, n_tensor * width), bf16),
+            pltpu.VMEM((rows, piece_rows), f32),
             pltpu.VMEM((2, n_tensor, tokens, width), bf16),
             pltpu.VMEM((2, n_layer, 2 * rows, piece_rows), bf16),
             pltpu.VMEM((2, CHUNKS, hops, rows, piece_rows), bf16),
@@ -712,12 +789,13 @@
             pltpu.VMEM((n_dp, rank // 2, lanes), f32),
             pltpu.VMEM((n_dp, 1, n_queries), f32),
             pltpu.VMEM((hops, 1, n_queries), f32),
+            pltpu.VMEM((1, n_queries), f32),
             dma((RAW,)),
             dma((CHUNKS,)),
-            dma((4,)),
+            dma((5,)),
             dma((2, CHUNKS, n_tensor - 1)),
             dma((2, CHUNKS, n_tensor - 1)),
-            dma((2, n_tensor - 1)),
+            dma((FIRST, n_tensor - 1)),
             dma((2, 2, n_layer)),
             dma((2, CHUNKS, hops)),
             dma((2, CHUNKS, hops)),
@@ -749,6 +827,7 @@
         proj_out,
         query_grads[0],
     )
+    return hand_over(*results)
 
 
 def solution(mesh):

time: 295 us -> 293 us (level)
  local copies, waits for them, and re-layouts: 3.38 us -> 0 us
    unnamed x2 -> x0, local copies, waits for them, and re-layouts: 3.38 us -> none
where the time goes in v4:
time: 293 us; the launch traced here: 292 us
  Pallas kernels  292 us (100%)
    pallas_call x1, Pallas kernels, on_device(): pl.pallas_call(functools.partial(stack_kernel, (layers, n_layer, n_tensor...  290 us

profile of v4, /device:TPU:0, one launch (start us, length us, event | category | flops | bytes accessed | tf_op | source)
XLA Modules:
  0.0 292.3 jit_solution(13289415786988711103)
XLA Ops:
  0.6 289.7 %backward_stack.1 = (bf16[512,1024]{1,0:T(8,128)(2,1)}, f32[1,128]{1,0:T(1,128)}) custom-call(s32[4]{0:T(128)} %owner_ref.1, bf16[512,1024]{1,0:T(8,128)(2,1)} %grad_hbm.1, bf16[4,4096,2,1024]{3,2,1,0:T(2,128)(2,1)} %bitcast.weight_hbm, bf16[4,512,1024]{2,1,0:T(8,128)(2,1)} %saved_hbm.1, bf16[2,128,1024]{2,1,0:T(8,128)(2,1)} %bitcast.4, ...), custom_call_target="tpu_custom_call" | custom-call | tf_op jit(solution)/shard_map/backward_stack/pallas_call | solution.py:753
  290.3 2.0 hand_over.1

commit v5 on v4

--- a/solution.py
+++ b/solution.py
@@ -54,6 +54,7 @@
     tensor_send,
     tensor_recv,
     seq_blocks,
+    flat_blocks,
     score_send,
     score_recv,
     score_total,
@@ -240,6 +241,8 @@
                 part[slot, q, here, at] = acc.astype(bf16)
 
             send_piece(slot, level, 0, q, k * first_rows, first_rows)
+            ready = blocks * k // FIRST
+            relay(blocks + ready, blocks * (k + 1) // FIRST - ready)
 
     def forward(slot, level, c, s):
         right_piece, left_piece = last - s + z, s - last + z
@@ -307,6 +310,11 @@
         @pl.when(level == 0)
         def _():
             out_copy(c).start()
+
+    def begin_total():
+        for k in range(CHUNKS):
+            total[k] = feats[(layers - 1) % 2, t, span(k), :].astype(f32)
+            project(layers - 1, k)
 
     def saved_copy(level):
         return pltpu.make_async_copy(saved_hbm.at[level], saved, load_sem.at[3])
@@ -507,15 +515,11 @@
         for shift in range(1, n_dp):
             seq_copy(shift).wait()
         pltpu.make_async_copy(query_hbm, queries, load_sem.at[2]).wait()
-        acc = None
         for j in range(rank // 2):
-            term = lax.dot_general(
-                seq_blocks[:, j, :].astype(bf16),
-                queries[:, j * lanes : (j + 1) * lanes],
-                NT,
-                preferred_element_type=f32,
-            )
-            acc = term if acc is None else acc + term
+            flat_blocks[:, j * lanes : (j + 1) * lanes] = seq_blocks[:, j, :]
+        acc = lax.dot_general(
+            flat_blocks[...].astype(bf16), queries[...], NT, preferred_element_type=f32
+        )
         for k in range(n_dp):
             score_send[k] = acc[k : k + 1]
         for shift in range(1, n_layer):
@@ -584,7 +588,7 @@
             def _():
                 task(*args)
 
-        @pl.when(p > 0)
+        @pl.when(p > 1)
         def _():
             forward(old_slot, old_level, old_c, 1)
 
@@ -595,9 +599,14 @@
 
             @pl.loop(1, n_layer)
             def _(i):
-                relay(i * blocks, blocks)
+                @pl.when(i > 1)
+                def _():
+                    relay(i * blocks, blocks)
+
                 multiply(slot, level, nth_piece(i), pl.ds(0, rows), pl.ds(0, rows))
                 send_piece(slot, level, 0, nth_piece(i))
+
+            forward(slot, level, 0, 1)
 
         @pl.when(p == 1)
         def _():
@@ -624,9 +633,12 @@
             def _(i):
                 q = nth_piece(i)
                 multiply(slot, level, q, span(c, 2), pl.ds(0, 2 * rows))
-                send_piece(slot, level, c, q)
-
-                @pl.when(p == phases - 2)
+
+                @pl.when((p < phases - 2) | (i < n_layer - 2))
+                def _():
+                    send_piece(slot, level, c, q)
+
+                @pl.when((p == phases - 2) & (i < n_layer - 2))
                 def _():
                     send_piece(slot, level, c + 1, q)
 
@@ -635,24 +647,23 @@
                 for i in range(n_layer):
                     send_piece(slot, level, c + 1, nth_piece(i))
 
-        base = (layers - level) * per_level + c * 2 * fraction
-        early = jnp.where(p == 1, 2 * fraction, jnp.where(c % 2 == 1, fraction, 0))
-        late = jnp.where((p == 1) | (c % 2 == 0), 2 * fraction, fraction)
+        top = level == layers - 1
+        base = (layers - level) * per_level + 2 * fraction * c
+        base = jnp.where(top, base - jnp.where(c == CHUNKS - 1, 1, 2) * fraction, base)
+        early = jnp.where((c % 2 == 1) & (p > 1), fraction, 0)
+        late = jnp.where(top & (c > 1), 3 * fraction, 2 * fraction) - early
+
         @pl.when(p == 0)
         def _():
             pltpu.make_async_copy(proj_out_hbm, proj_out, load_sem.at[0]).wait()
             pltpu.make_async_copy(proj_in_hbm, proj_in, load_sem.at[1]).wait()
             pltpu.make_async_copy(query_hbm, queries, load_sem.at[2]).start()
             saved_copy(0).start()
-            for k in range(CHUNKS):
-                total[k] = feats[(layers - 1) % 2, t, span(k), :].astype(f32)
-                project(layers - 1, k)
-
         at_phase(phases - 3, send_blocks)
 
         @pl.when((p > 0) & (level > 0))
         def _():
-            relay(jnp.where(p == 1, per_level, base), early)
+            relay(base, early)
 
         for s in range(2, n_layer - 1):
 
@@ -660,15 +671,15 @@
             def _():
                 forward(old_slot, old_level, old_c, s)
 
+        at_phase(1, begin_total)
         for k in range(layers):
             at_phase(CHUNKS + k, project_saved, k)
         for k in range(n_layer):
-            at_phase(CHUNKS + layers + k, run_step, k)
-        at_phase(phases - 2, sum_layers)
+            at_phase(CHUNKS + layers + 1 + k, run_step, k)
 
         @pl.when((p > 0) & (level > 0))
         def _():
-            relay(base + 2 * fraction - late, late)
+            relay(base + early, late)
 
         @pl.when(p > 0)
         def _():
@@ -677,12 +688,17 @@
 
     end_slot, end_level = ((phases - 1) // 2) % 2, jnp.int32(0)
     pair = (CHUNKS - 2, CHUNKS - 1)
+    def score_and_send():
+        score()
+        for c in pair:
+            send_piece(end_slot, end_level, c, nth_piece(n_layer - 2))
+
+    between = [sum_layers, sum_tensor, score_and_send]
     for s in range(1, last):
         for c in pair:
             forward(end_slot, end_level, c, s)
-        if s == 1:
-            sum_tensor()
-    score()
+            if between:
+                between.pop(0)()
     for c in pair:
         forward(end_slot, end_level, c, last)
         finish(end_slot, end_level, c)
@@ -787,6 +803,7 @@
             pltpu.VMEM((rank // 2, lanes), f32),
             pltpu.VMEM((n_tensor - 1, rank // 2, lanes), f32),
             pltpu.VMEM((n_dp, rank // 2, lanes), f32),
+            pltpu.VMEM((n_dp, rank * rank), f32),
             pltpu.VMEM((n_dp, 1, n_queries), f32),
             pltpu.VMEM((hops, 1, n_queries), f32),
             pltpu.VMEM((1, n_queries), f32),

time: 293 us -> 289 us (0.986)
  Pallas kernels: 292 us -> 286 us
    pallas_call x1, Pallas kernels: 290 us -> 284 us  [on_device(): pl.pallas_call(functools.partial(stack_kernel, (layers, n_layer, n_tensor...]
where the time goes in v5:
time: 289 us; the launch traced here: 287 us
  Pallas kernels  286 us (99%)
    pallas_call x1, Pallas kernels, on_device(): pl.pallas_call(functools.partial(stack_kernel, (layers, n_layer, n_tensor...  284 us

profile of v5, /device:TPU:0, one launch (start us, length us, event | category | flops | bytes accessed | tf_op | source)
XLA Modules:
  0.0 286.7 jit_solution(9695786861965327505)
XLA Ops:
  0.6 284.1 %backward_stack.1 = (bf16[512,1024]{1,0:T(8,128)(2,1)}, f32[1,128]{1,0:T(1,128)}) custom-call(s32[4]{0:T(128)} %owner_ref.1, bf16[512,1024]{1,0:T(8,128)(2,1)} %grad_hbm.1, bf16[4,4096,2,1024]{3,2,1,0:T(2,128)(2,1)} %bitcast.weight_hbm, bf16[4,512,1024]{2,1,0:T(8,128)(2,1)} %saved_hbm.1, bf16[2,128,1024]{2,1,0:T(8,128)(2,1)} %bitcast.4, ...), custom_call_target="tpu_custom_call" | custom-call | tf_op jit(solution)/shard_map/backward_stack/pallas_call | solution.py:769
  284.7 2.0 hand_over.1
